TPU v7x, 128 devices: a whole 4x4x4 slice. The times are simulated.
128 devices in a mesh: freq: 8 (over y_hi, z), src: 16 (over y_lo, x, core).
Axes of the slice: x: 4, y: 4 (y_hi: 2, y_lo: 2; y = y_hi * 2 + y_lo), z: 4, core: 2. Of those that a mesh axis runs over, the one named last changes fastest.
Arguments:
- reflection: bfloat16 [2, 128, 2048, 2048], P(None, 'freq', None, 'src'), may hold values from -0.125 to 0.125
- direct_wave: float32 [2048, 128, 128], P('src', 'freq'), may hold values from -6 to 6
- first_arrival: int32 [2048, 64], P(('src', 'freq')), may hold values from 64 to 191
Outputs:
- focus_minus: float32 [2048, 128, 128], P('src', 'freq')
- focus_plus: float32 [2048, 128, 128], P('src', 'freq')
All inputs are finite; a program needn't handle non-finite values.
Results may differ from a plain program's by a relative error of at most 0.035.
Values may be sent and summed in bfloat16 or wider, within the bound.
A program may use at most 128 MiB of HBM per device.

v0:
```python
import math

import jax
import jax.numpy as jnp
from jax import lax
from jax.sharding import PartitionSpec as P

NT = 512
ITERS = 2


def transform_tables(nfreq, ntime):
    freqs = jnp.arange(1, nfreq + 1, dtype=jnp.int32)
    times = jnp.arange(ntime, dtype=jnp.int32)
    phase = (freqs[:, None] * times[None, :] % ntime).astype(jnp.float32) * (2.0 * math.pi / ntime)
    cosine = jnp.cos(phase)
    sine = jnp.sin(phase)
    inverse = jnp.stack([cosine * (2.0 / ntime), -sine * (2.0 / ntime)]).astype(jnp.bfloat16)
    forward = jnp.stack([cosine, -sine]).astype(jnp.bfloat16)
    return (inverse, forward)


def apply_window(spectrum, first_arrival, inverse, forward):
    rows_count, nfreq, width = spectrum.shape
    half = width // 2
    ntime = inverse.shape[2]
    split = spectrum.reshape(rows_count, nfreq, 2, half)
    signal = jnp.einsum("rfpc,pft->rct", split, inverse, preferred_element_type=jnp.float32)
    times = jnp.arange(ntime, dtype=jnp.int32)
    limit = first_arrival[:, :, None]
    keep = (times[None, None, :] < limit) | (times[None, None, :] > ntime - limit)
    windowed = jnp.where(keep, signal, jnp.zeros_like(signal)).astype(jnp.bfloat16)
    back = jnp.einsum("rct,pft->rfpc", windowed, forward, preferred_element_type=jnp.float32)
    return back.reshape(rows_count, nfreq, width)


def stacked_parts(vectors, factor):
    rounded = vectors.astype(jnp.bfloat16)
    half = rounded.shape[-1] // 2
    swapped = jnp.concatenate([-rounded[..., half:], rounded[..., :half]], axis=-1)
    if factor < 0:
        swapped = -swapped
    return jnp.stack([rounded, swapped])


def to_owners(reflection, vectors, factor):
    operand = stacked_parts(vectors, factor)
    summed = lax.psum_scatter(
        jnp.einsum(
            "pfrs,psfk->rfk", reflection, operand, preferred_element_type=jnp.float32
        ).astype(jnp.bfloat16),
        "src",
        scatter_dimension=0,
        tiled=True,
    )
    return lax.all_to_all(summed, "freq", split_axis=0, concat_axis=1, tiled=True)


def to_groups(spectrum):
    return lax.all_to_all(
        spectrum.astype(jnp.bfloat16), "freq", split_axis=1, concat_axis=0, tiled=True
    ).astype(spectrum.dtype)


def local(reflection, direct_wave, first_arrival):
    nfreq = direct_wave.shape[1] * lax.axis_size("freq")
    inverse, forward = transform_tables(nfreq, NT)
    focus_plus = direct_wave
    focus_minus = direct_wave
    for iteration in range(ITERS):
        spectrum = to_owners(reflection, focus_plus, 1.0)
        focus_minus = to_groups(apply_window(spectrum, first_arrival, inverse, forward))
        spectrum = to_owners(reflection, focus_minus, -1.0)
        update = to_groups(apply_window(spectrum, first_arrival, inverse, forward))
        focus_plus = direct_wave + update
    return (focus_minus, focus_plus)


def solution(mesh):
    in_specs = (P(None, "freq", None, "src"), P("src", "freq", None), P(("src", "freq"), None))
    out_specs = (P("src", "freq", None), P("src", "freq", None))
    return jax.shard_map(local, mesh=mesh, in_specs=in_specs, out_specs=out_specs, check_vma=False)
```

profile of v0, /device:TPU:0, one launch (start us, length us, event | category | flops | bytes accessed | tf_op | source)
XLA Modules:
  0.0 548.1 jit_solution(8581948061272657369)
XLA Ops:
  7.2 1.6 copy.115
  9.1 11.0 %bitcast_convert_fusion.3 = bf16[16,128,2048]{2,1,0:T(8,128)(2,1)} fusion(bf16[2,16,2048,128]{3,2,1,0:T(8,128)(2,1)} %param.3, bf16[1,128,16,128]{1,3,0,2:T(8,128)(2,1)S(1)} %maximum_bitcast_fusion, bf16[1,128,16,128]{1,3,0,2:T(8,128)(2,1)S(1)} %convert_bitcast_fusion.2), kind=kOutput, calls=%fused_computation.3 | convolution fusion | flops 2152202240 | bytes 26214400 | tf_op jit(solution)/shard_map/pfrs,psfk->rfk/dot_general | solution.py:49
  20.1 12.3 %copy.159 = bf16[2048,2048]{1,0:T(8,128)(2,1)} copy(bf16[2048,2048]{0,1:T(8,128)(2,1)} %bitcast.177) | data formatting | bytes 16777216
  32.4 77.2 %reduce-scatter.13.cloned.1.call-done = bf16[128,2048]{1,0:T(8,128)(2,1)} async-done(((bf16[2048,2048]{1,0:T(8,128)(2,1)}), bf16[128,2048]{1,0:T(8,128)(2,1)}) %reduce-scatter.13.cloned.1.call-update) | async-done | bytes 524304
  109.6 1.3 copy.160
  110.9 1.2 copy.96
  112.1 6.6 %all-to-all-start = ((bf16[128,16,128]{2,1,0:T(8,128)(2,1)}), bf16[128,16,128]{2,1,0:T(8,128)(2,1)S(1)}, u32[]{:S(2)}, u32[]{:S(2)}) async-start(bf16[128,16,128]{2,1,0:T(8,128)(2,1)} %copy.96), calls=%async_computation | async-start | bytes 1048576 | tf_op jit(solution)/shard_map/all_to_all | solution.py:56
  118.8 1.9 fusion.69
  120.7 7.8 %all-to-all-done = bf16[128,16,128]{2,1,0:T(8,128)(2,1)S(1)} async-done(((bf16[128,16,128]{2,1,0:T(8,128)(2,1)}), bf16[128,16,128]{2,1,0:T(8,128)(2,1)S(1)}, u32[]{:S(2)}, u32[]{:S(2)}) %all-to-all-start) | async-done | bytes 524320 | tf_op jit(solution)/shard_map/all_to_all | solution.py:56
  128.6 0.4 reshape.255
  129.0 1.8 fusion.25
  130.9 0.4 copy.100
  131.3 13.1 %all_to_all.114 = bf16[16,128,128]{2,0,1:T(8,128)(2,1)S(1)} all-to-all(bf16[16,128,128]{2,0,1:T(8,128)(2,1)S(1)} %copy.100), channel_id=1, replica_groups=mesh['freq'=8,'src'=16] {'freq'}, dimensions={1} | all-to-all | bytes 1048576 | tf_op jit(solution)/shard_map/all_to_all | solution.py:60
  144.4 0.1 copy.102
  144.5 0.5 copy.106
  145.0 0.2 fusion.79
  145.2 0.5 copy.167
  145.7 0.5 copy.168
  146.2 0.1 maximum_negate_fusion
  146.3 11.0 %bitcast_convert_fusion.2 = bf16[16,128,2048]{2,1,0:T(8,128)(2,1)} fusion(bf16[2,16,2048,128]{3,2,1,0:T(8,128)(2,1)} %param.3, bf16[1,128,16,128]{1,3,0,2:T(8,128)(2,1)S(1)} %maximum_negate_fusion, bf16[1,128,16,128]{1,3,0,2:T(8,128)(2,1)S(1)} %copy.106), kind=kOutput, calls=%fused_computation.2 | convolution fusion | flops 2152202240 | bytes 26214400 | tf_op jit(solution)/shard_map/pfrs,psfk->rfk/dot_general | solution.py:49
  157.3 12.3 %copy.161 = bf16[2048,2048]{1,0:T(8,128)(2,1)} copy(bf16[2048,2048]{0,1:T(8,128)(2,1)} %bitcast.178) | data formatting | bytes 16777216
  169.7 71.8 %reduce-scatter.15.cloned.1.call-done = bf16[128,2048]{1,0:T(8,128)(2,1)} async-done(((bf16[2048,2048]{1,0:T(8,128)(2,1)}), bf16[128,2048]{1,0:T(8,128)(2,1)}) %reduce-scatter.15.cloned.1.call-update) | async-done | bytes 524304
  241.4 1.3 copy.162
  242.7 0.4 copy.108
  243.2 16.5 %all_to_all.115 = bf16[128,16,128]{2,1,0:T(8,128)(2,1)S(1)} all-to-all(bf16[128,16,128]{2,1,0:T(8,128)(2,1)S(1)} %copy.108), channel_id=1, replica_groups=mesh['freq'=8,'src'=16] {'freq'}, dimensions={0} | all-to-all | bytes 1048576 | tf_op jit(solution)/shard_map/all_to_all | solution.py:56
  259.7 0.4 reshape.256
  260.1 1.8 fusion.26
  262.0 0.4 copy.112
  262.4 12.7 %all_to_all.116 = bf16[16,128,128]{2,0,1:T(8,128)(2,1)S(1)} all-to-all(bf16[16,128,128]{2,0,1:T(8,128)(2,1)S(1)} %copy.112), channel_id=1, replica_groups=mesh['freq'=8,'src'=16] {'freq'}, dimensions={1} | all-to-all | bytes 1048576 | tf_op jit(solution)/shard_map/all_to_all | solution.py:60
  275.2 0.1 copy.113
  275.4 1.1 copy.114
  276.5 1.6 copy.116
  278.1 0.1 add_convert_fusion
  278.3 11.0 %bitcast_convert_fusion.1 = bf16[16,128,2048]{2,1,0:T(8,128)(2,1)} fusion(bf16[2,16,2048,128]{3,2,1,0:T(8,128)(2,1)} %param.3, bf16[1,128,16,128]{1,3,0,2:T(8,128)(2,1)S(1)} %maximum_bitcast_fusion.1, bf16[1,128,16,128]{1,3,0,2:T(8,128)(2,1)S(1)} %bitcast.185), kind=kOutput, calls=%fused_computation.1 | convolution fusion | flops 2152202240 | bytes 26214400 | tf_op jit(solution)/shard_map/pfrs,psfk->rfk/dot_general | solution.py:49
  289.3 12.3 %copy.163 = bf16[2048,2048]{1,0:T(8,128)(2,1)} copy(bf16[2048,2048]{0,1:T(8,128)(2,1)} %bitcast.179) | data formatting | bytes 16777216
  301.7 71.6 %reduce-scatter.17.cloned.1.call-done = bf16[128,2048]{1,0:T(8,128)(2,1)} async-done(((bf16[2048,2048]{1,0:T(8,128)(2,1)}), bf16[128,2048]{1,0:T(8,128)(2,1)}) %reduce-scatter.17.cloned.1.call-update) | async-done | bytes 524304
  373.3 1.3 copy.164
  374.6 0.4 copy.119
  375.1 16.6 %all_to_all.117 = bf16[128,16,128]{2,1,0:T(8,128)(2,1)S(1)} all-to-all(bf16[128,16,128]{2,1,0:T(8,128)(2,1)S(1)} %copy.119), channel_id=1, replica_groups=mesh['freq'=8,'src'=16] {'freq'}, dimensions={0} | all-to-all | bytes 1048576 | tf_op jit(solution)/shard_map/all_to_all | solution.py:56
  391.8 0.4 reshape.257
  392.2 0.9 fusion.27
  393.2 0.4 copy.123
  393.6 12.7 %all_to_all.118 = bf16[16,128,128]{2,0,1:T(8,128)(2,1)S(1)} all-to-all(bf16[16,128,128]{2,0,1:T(8,128)(2,1)S(1)} %copy.123), channel_id=1, replica_groups=mesh['freq'=8,'src'=16] {'freq'}, dimensions={1} | all-to-all | bytes 1048576 | tf_op jit(solution)/shard_map/all_to_all | solution.py:60
  406.3 0.1 copy.125
  406.5 0.5 copy.129
  406.9 0.2 fusion.78
  407.2 0.5 copy.169
  407.7 0.5 copy.170
  408.1 0.1 maximum_negate_fusion.1
  408.3 11.0 %bitcast_convert_fusion = bf16[16,128,2048]{2,1,0:T(8,128)(2,1)} fusion(bf16[2,16,2048,128]{3,2,1,0:T(8,128)(2,1)} %param.3, bf16[1,128,16,128]{1,3,0,2:T(8,128)(2,1)S(1)} %maximum_negate_fusion.1, bf16[1,128,16,128]{1,3,0,2:T(8,128)(2,1)S(1)} %copy.129), kind=kOutput, calls=%fused_computation | convolution fusion | flops 2152202240 | bytes 26214400 | tf_op jit(solution)/shard_map/pfrs,psfk->rfk/dot_general | solution.py:49
  419.3 12.3 %copy.165 = bf16[2048,2048]{1,0:T(8,128)(2,1)} copy(bf16[2048,2048]{0,1:T(8,128)(2,1)} %bitcast.180) | data formatting | bytes 16777216
  431.6 71.6 %reduce-scatter.19.cloned.1.call-done = bf16[128,2048]{1,0:T(8,128)(2,1)} async-done(((bf16[2048,2048]{1,0:T(8,128)(2,1)}), bf16[128,2048]{1,0:T(8,128)(2,1)}) %reduce-scatter.19.cloned.1.call-update) | async-done | bytes 524304
  503.2 1.3 copy.166
  504.5 0.4 copy.131
  505.0 16.5 %all_to_all.119 = bf16[128,16,128]{2,1,0:T(8,128)(2,1)S(1)} all-to-all(bf16[128,16,128]{2,1,0:T(8,128)(2,1)S(1)} %copy.131), channel_id=1, replica_groups=mesh['freq'=8,'src'=16] {'freq'}, dimensions={0} | all-to-all | bytes 1048576 | tf_op jit(solution)/shard_map/all_to_all | solution.py:56
  521.5 0.4 reshape.258
  521.9 2.6 fusion.28
  524.6 1.1 copy.134
  525.6 1.2 copy.135
  526.8 3.5 all-to-all-start.7
  530.3 1.1 bitcast_convert_fusion.4
  531.4 8.6 %all-to-all-done.7 = bf16[16,128,128]{2,0,1:T(8,128)(2,1)S(1)} async-done(((bf16[16,128,128]{2,0,1:T(8,128)(2,1)}), bf16[16,128,128]{2,0,1:T(8,128)(2,1)S(1)}, u32[]{:S(2)}, u32[]{:S(2)}) %all-to-all-start.7) | async-done | bytes 524320 | tf_op jit(solution)/shard_map/all_to_all | solution.py:60
  540.1 0.1 copy.136
  540.4 1.1 bitcast_add_fusion
  (34 shorter events, 1.3 us)
Async XLA Ops:
  7.2 102.5 %reduce-scatter.13.cloned.1.call-start = ((), (), s32[]{:S(2)}) async-start(), calls=%async_computation.12 | async-start | bytes 8912896
  32.4 86.4 %copy-start.2 = (s32[16,64]{1,0:T(8,128)S(1)}, s32[16,64]{1,0:T(8,128)}, u32[]{:S(2)}) copy-start(s32[16,64]{1,0:T(8,128)} %param.5) | copy-start | bytes 12292
  112.1 16.4 %all-to-all-start = ((bf16[128,16,128]{2,1,0:T(8,128)(2,1)}), bf16[128,16,128]{2,1,0:T(8,128)(2,1)S(1)}, u32[]{:S(2)}, u32[]{:S(2)}) async-start(bf16[128,16,128]{2,1,0:T(8,128)(2,1)} %copy.96), calls=%async_computation | async-start | bytes 1048576 | tf_op jit(solution)/shard_map/all_to_all | solution.py:56
  118.7 122.7 %reduce-scatter.15.cloned.1.call-start = ((), (), s32[]{:S(2)}) async-start(), calls=%async_computation.13 | async-start | bytes 8912896
  169.6 203.7 %reduce-scatter.17.cloned.1.call-start = ((), (), s32[]{:S(2)}) async-start(), calls=%async_computation.14 | async-start | bytes 8912896
  301.6 90.6 %copy-start.1 = (bf16[1,128,512]{2,1,0:T(8,128)(2,1)S(1)}, bf16[1,128,512]{2,1,0:T(8,128)(2,1)}, u32[]{:S(2)}) copy-start(bf16[1,128,512]{2,1,0:T(8,128)(2,1)} %get-tuple-element.15) | copy-start | bytes 393220
  301.6 201.6 %reduce-scatter.19.cloned.1.call-start = ((), (), s32[]{:S(2)}) async-start(), calls=%async_computation.15 | async-start | bytes 8912896
  521.5 18.9 %copy-start = (f32[128,16,128]{2,1,0:T(8,128)S(1)}, f32[128,16,128]{2,1,0:T(8,128)}, u32[]{:S(2)}) copy-start(f32[128,16,128]{2,1,0:T(8,128)} %param.4) | copy-start | bytes 3145732
  526.8 13.2 %all-to-all-start.7 = ((bf16[16,128,128]{2,0,1:T(8,128)(2,1)}), bf16[16,128,128]{2,0,1:T(8,128)(2,1)S(1)}, u32[]{:S(2)}, u32[]{:S(2)}) async-start(bf16[16,128,128]{2,0,1:T(8,128)(2,1)} %copy.135), calls=%async_computation.7 | async-start | bytes 1048576 | tf_op jit(solution)/shard_map/all_to_all | solution.py:60
Sparse Core Ops, SparseCore 0:
  32.5 77.0 reduce-scatter.12
  169.7 71.6 reduce-scatter.14
  301.7 71.5 reduce-scatter.16
  431.7 71.4 reduce-scatter.18
where the time goes:
time: 550 us; the launch traced here: 548 us
  waiting for transfers between devices  309 us (56%)
  blocking collectives  88.1 us (16%)
  local copies, waits for them, and re-layouts  70.4 us (13%)
  matrix products  51.2 us (9%)
  between operations  14.2 us (3%)
  starting transfers between devices  10.3 us (2%)
    unnamed x8, waiting for transfers between devices  292 us
    unnamed x19, local copies, waits for them, and re-layouts  57.8 us
    all_to_all x3, blocking collectives, to_owners(): lax.all_to_all(summed, 'freq', split_axis=0, concat_axis=1, tiled=True)  49.6 us
    dot_general x4, matrix products, to_owners(): jnp.einsum('pfrs,psfk->rfk', reflection, operand, preferred_element_type=...  44 us
    all_to_all x3, blocking collectives, to_groups(): lax.all_to_all(spectrum.astype(jnp.bfloat16), 'freq', split_axis=1, conca...  38.5 us
  transfers between devices with their start and end apart: 6, of which 6 were waited for; matrix products, arithmetic and copies ran while one was open for 1% of the time, Pallas kernels for 0%

commit v1 on v0

v1 whole, which is shorter than its diff:
```python
import functools
import math

import jax
import jax.numpy as jnp
import ml_dtypes
import numpy as np
from jax import lax
from jax.experimental import pallas as pl
from jax.experimental.pallas import tpu as pltpu
from jax.sharding import PartitionSpec as P

NT = 512
ITERS = 2
APPS = 2 * ITERS
NFREQ = 128
PEERS = 8
FDEV = 16
PAIRS = FDEV // 2
BLOCK = 128
C4 = 4
ROWS = 64
CUT = 192
TS = 2 * CUT
TICKS = APPS * 2 * PAIRS
MESH = pl.DeviceIdType.MESH
BF = jnp.bfloat16
F32 = jnp.float32


def tables():
    freqs = np.arange(1, NFREQ + 1, dtype=np.int32)
    times = np.concatenate([np.arange(CUT), np.arange(NT - CUT, NT)]).astype(np.int32)
    phase = ((freqs[:, None] * times[None, :]) % NT).astype(np.float32) * np.float32(2.0 * math.pi / NT)
    cosine, sine = np.cos(phase), np.sin(phase)
    inverse = np.stack([cosine * np.float32(2.0 / NT), -sine * np.float32(2.0 / NT)]).astype(ml_dtypes.bfloat16)
    forward = np.stack([cosine, -sine]).astype(ml_dtypes.bfloat16)
    inv = np.zeros((C4, TS, NFREQ, 2, C4), ml_dtypes.bfloat16)
    fwd = np.zeros((NFREQ, 2, C4, C4, TS), ml_dtypes.bfloat16)
    for c in range(C4):
        inv[c, :, :, :, c] = inverse.transpose(2, 1, 0)
        fwd[:, :, c, c, :] = forward.transpose(1, 0, 2)
    return inv.reshape(C4 * TS, NFREQ * 2 * C4), fwd.reshape(NFREQ * 2 * C4, C4 * TS)


def kernel(r_hbm, dw, fa, inv_hbm, fwd_hbm, out,
           r, inv, fwd, w, p, c_in, t, a_in, b_in, u, y_in, f, g_in, h, v_in, fa_in, wn,
           ss, rs, gss, grs, hss, hrs, fss, frs, lsem, tsem):
    me = lax.axis_index("freq")
    src = lax.axis_index("src")
    core = lax.rem(src, 2)
    x = lax.rem(src // 2, 4)
    y = src // 8

    def at_src(yy, xx, cc):
        return (me, (yy * 4 + xx) * 2 + cc)

    right = lax.rem(x + 1, 4)
    left = lax.rem(x + 3, 4)
    to_core = at_src(y, x, 1 - core)
    to_right = at_src(y, right, core)
    to_left = at_src(y, left, core)
    to_y = at_src(1 - y, x, core)
    peers = [lax.rem(me + i, PEERS) for i in range(1, PEERS)]

    def load_r(k):
        part = pl.ds(2 * k, 2)
        return pltpu.make_async_copy(r_hbm.at[:, part], r.at[:, part], lsem.at[k])

    def load_tables():
        return (pltpu.make_async_copy(inv_hbm, inv, tsem.at[0]), pltpu.make_async_copy(fwd_hbm, fwd, tsem.at[1]))

    for k in range(PAIRS):
        load_r(k).start()
    for copy in load_tables():
        copy.start()

    barrier = pltpu.get_barrier_semaphore()
    for d in [to_core, to_right, to_left, to_y] + [(q, src) for q in peers]:
        pl.semaphore_signal(barrier, inc=1, device_id=d, device_id_type=MESH)
    pl.semaphore_wait(barrier, 4 + PEERS - 1)

    def remote(source, target, send, recv, device):
        return pltpu.make_async_remote_copy(
            src_ref=source, dst_ref=target, send_sem=send, recv_sem=recv, device_id=device, device_id_type=MESH)

    def core_copy(k):
        s = lax.rem(k, 2)
        return remote(p.at[s, 1 - core], c_in.at[s], ss.at[0, s], rs.at[0, s], to_core)

    def a_copies(k):
        s = lax.rem(k, 2)
        return (remote(t.at[s, 2, 0], a_in.at[s, 0], ss.at[1, s], rs.at[1, s], to_right),
                remote(t.at[s, 2, 1], a_in.at[s, 1], ss.at[2, s], rs.at[2, s], to_left))

    def b_copies(k):
        s = lax.rem(k, 2)
        return (remote(t.at[s, 1], b_in.at[s, 0], ss.at[3, s], rs.at[3, s], to_right),
                remote(t.at[s, 3], b_in.at[s, 1], ss.at[4, s], rs.at[4, s], to_left))

    def y_copy(k):
        s = lax.rem(k, 2)
        return remote(u.at[s, 1], y_in.at[s], ss.at[5, s], rs.at[5, s], to_y)

    def fa_copy(i):
        return remote(fa.at[peers[i]], fa_in.at[me], fss.at[i], frs.at[i], (peers[i], src))

    def g_copy(half, i):
        return remote(f.at[half, peers[i]], g_in.at[half, me], gss.at[half, i], grs.at[half, i], (peers[i], src))

    def h_copy(half, i):
        return remote(h.at[half, peers[i]], v_in.at[half, me], hss.at[half, i], hrs.at[half, i], (peers[i], src))

    for i in range(PEERS - 1):
        fa_copy(i).start()
    fa_in[me] = fa[me]

    row = lax.broadcasted_iota(jnp.int32, (PEERS, 2 * C4, BLOCK), 1)

    def stack_rows(half, value, pair, sign):
        for q in range(2):
            part = value[:, 8 * q:8 * q + 8, :]
            turned = jnp.concatenate(
                [jnp.concatenate([part[i, 4:8], part[i, 0:4]], axis=0)[None] for i in range(PEERS)], axis=0)
            turned = jnp.where(row < C4, -sign * turned, sign * turned)
            w[half, 2 * pair + q, :, 0:BLOCK] = part.reshape(ROWS, BLOCK).astype(BF)
            w[half, 2 * pair + q, :, BLOCK:2 * BLOCK] = turned.reshape(ROWS, BLOCK).astype(BF)

    def first_rows(i, _):
        half, pair = i // PAIRS, lax.rem(i, PAIRS)
        stack_rows(half, dw[half, :, pair], pair, 1.0)
        return _

    lax.fori_loop(0, 2 * PAIRS, first_rows, 0)

    def matmul(k):
        s = lax.rem(k, 2)
        pair = lax.rem(k, PAIRS)
        half = lax.rem(k // PAIRS, 2)
        for q in range(2):
            freq = 2 * pair + q
            lhs = w[half, freq]
            for xr in range(4):
                for yr in range(2):
                    yy = y if yr == 0 else 1 - y
                    start = pl.multiple_of((yy * 4 + lax.rem(x + xr, 4)) * 2 * BLOCK, 2 * BLOCK)
                    rows = pl.ds(start, 2 * BLOCK)
                    rhs = jnp.concatenate([r[0, freq, rows, :], r[1, freq, rows, :]], axis=1)
                    term = lax.dot_general(lhs, rhs, (((1,), (1,)), ((), ())), preferred_element_type=F32).astype(BF)
                    p[s, 0, xr, yr, q] = term[:, 0:BLOCK]
                    p[s, 1, xr, yr, q] = term[:, BLOCK:2 * BLOCK]

    def window(n):
        half = lax.rem(n, 2)
        for i in range(PEERS - 1):
            g_copy(half, i).wait()
        spectrum = g_in[half].reshape(NFREQ * 2 * C4, BLOCK)
        time = lax.broadcasted_iota(jnp.int32, (TS, BLOCK), 0)
        time = jnp.where(time < CUT, time, time + (NT - TS)).astype(F32)
        for c in range(C4):
            signal = jnp.dot(inv[c * TS:(c + 1) * TS, :], spectrum, preferred_element_type=F32)
            limit = fa_in[0, pl.ds(half * C4 + c, 1), :]
            for q in range(1, PEERS):
                limit = limit + fa_in[q, pl.ds(half * C4 + c, 1), :]
            keep = (time < limit) | (time > NT - limit)
            wn[c * TS:(c + 1) * TS, :] = jnp.where(keep, signal, 0.0).astype(BF)
        for q in range(PEERS):
            back = jnp.dot(fwd[q * BLOCK:(q + 1) * BLOCK, :], wn[...], preferred_element_type=F32)
            h[half, q] = back.astype(BF).reshape(PAIRS, 16, BLOCK)
        v_in[half, me] = h[half, me]
        for i in range(PEERS - 1):
            h_copy(half, i).start()

    def update(n):
        half = lax.rem(n, 2)
        app = n // 2
        odd = lax.rem(app, 2)
        flag = odd.astype(F32)
        sign = 2.0 * flag - 1.0
        for i in range(PEERS - 1):
            h_copy(half, i).wait()

        def one(pair, _):
            value = v_in[half, :, pair].astype(F32) + flag * dw[half, :, pair]
            out[odd, half, :, pair] = value
            stack_rows(half, value, pair, sign)
            return _

        lax.fori_loop(0, PAIRS, one, 0)

    def tick(k, carry):
        @pl.when((k >= 4) & (k < TICKS + 4))
        def _():
            j = k - 4
            s = lax.rem(j, 2)
            pair = lax.rem(j, PAIRS)
            n = j // PAIRS
            half = lax.rem(n, 2)
            y_copy(j).wait()
            total = u[s, 0].astype(F32) + y_in[s].astype(F32)
            total = total.reshape(2, PEERS, 2 * C4, BLOCK)
            f[half, :, pair] = jnp.concatenate([total[0], total[1]], axis=1).astype(BF)

            @pl.when(pair == PAIRS - 1)
            def _():
                for i in range(PEERS - 1):
                    g_copy(half, i).start()
                g_in[half, me] = f[half, me]

        @pl.when((k >= 3) & (k < TICKS + 3))
        def _():
            j = k - 3
            s = lax.rem(j, 2)
            for copy in b_copies(j):
                copy.wait()
            u[s, 1] = (t[s, 0, 1].astype(F32) + b_in[s, 0, 1].astype(F32) + b_in[s, 1, 1].astype(F32)).astype(BF)
            y_copy(j).start()
            u[s, 0] = (t[s, 0, 0].astype(F32) + b_in[s, 0, 0].astype(F32) + b_in[s, 1, 0].astype(F32)).astype(BF)

        @pl.when((k >= 2) & (k < TICKS + 2))
        def _():
            j = k - 2
            s = lax.rem(j, 2)
            for copy in a_copies(j):
                copy.wait()
            t[s, 1, 0] = (t[s, 1, 0].astype(F32) + a_in[s, 0].astype(F32)).astype(BF)
            t[s, 3, 1] = (t[s, 3, 1].astype(F32) + a_in[s, 1].astype(F32)).astype(BF)
            for copy in b_copies(j):
                copy.start()

        @pl.when((k >= 1) & (k < TICKS + 1))
        def _():
            j = k - 1
            s = lax.rem(j, 2)
            core_copy(j).wait()
            for xr in (2, 1, 3, 0):
                t[s, xr] = (p[s, core, xr].astype(F32) + c_in[s, xr].astype(F32)).astype(BF)
                if xr == 2:
                    for copy in a_copies(j):
                        copy.start()

        @pl.when(k < PAIRS)
        def _():
            load_r(k).wait()

        @pl.when(k < TICKS)
        def _():
            matmul(k)
            core_copy(k).start()

        @pl.when(k == PAIRS)
        def _():
            for copy in load_tables():
                copy.wait()
            for i in range(PEERS - 1):
                fa_copy(i).wait()

        @pl.when((k >= 13) & (lax.rem(k, PAIRS) == 5))
        def _():
            window((k - 13) // PAIRS)

        @pl.when((k >= 15) & (lax.rem(k, PAIRS) == 7))
        def _():
            update((k - 15) // PAIRS)

        return carry

    lax.fori_loop(0, TICKS + PAIRS, tick, 0)


def local(reflection, direct_wave, first_arrival):
    me = lax.axis_index("freq")
    inv, fwd = tables()
    dw = direct_wave.reshape(BLOCK, PAIRS, 2, 2, 2, PEERS, C4)
    dw = dw.transpose(4, 5, 1, 2, 3, 6, 0).reshape(2, PEERS, PAIRS, 16, BLOCK)
    fa = first_arrival.astype(F32).reshape(16, 2, PEERS, C4).transpose(2, 1, 3, 0).reshape(PEERS, 2 * C4, 16)
    fa = jnp.where(jnp.arange(BLOCK) // 16 == me, jnp.tile(fa, (1, 1, PEERS)), 0.0)
    vmem = pl.BlockSpec(memory_space=pltpu.VMEM)
    hbm = pl.BlockSpec(memory_space=pl.ANY)
    dma = pltpu.SemaphoreType.DMA
    unit = (2, ROWS, BLOCK)
    out = pl.pallas_call(
        kernel,
        out_shape=jax.ShapeDtypeStruct((2, 2, PEERS, PAIRS, 16, BLOCK), F32),
        in_specs=[hbm, vmem, vmem, hbm, hbm],
        out_specs=vmem,
        scratch_shapes=[
            pltpu.VMEM(reflection.shape, BF),
            pltpu.VMEM(inv.shape, BF),
            pltpu.VMEM(fwd.shape, BF),
            pltpu.VMEM((2, FDEV, ROWS, 2 * BLOCK), BF),
            pltpu.VMEM((2, 2, 4, 2) + unit, BF),
            pltpu.VMEM((2, 4, 2) + unit, BF),
            pltpu.VMEM((2, 4, 2) + unit, BF),
            pltpu.VMEM((2, 2) + unit, BF),
            pltpu.VMEM((2, 2, 2) + unit, BF),
            pltpu.VMEM((2, 2) + unit, BF),
            pltpu.VMEM((2,) + unit, BF),
            pltpu.VMEM((2, PEERS, PAIRS, 16, BLOCK), BF),
            pltpu.VMEM((2, PEERS, PAIRS, 16, BLOCK), BF),
            pltpu.VMEM((2, PEERS, PAIRS, 16, BLOCK), BF),
            pltpu.VMEM((2, PEERS, PAIRS, 16, BLOCK), BF),
            pltpu.VMEM((PEERS, 2 * C4, BLOCK), F32),
            pltpu.VMEM((C4 * TS, BLOCK), BF),
            dma((6, 2)), dma((6, 2)),
            dma((2, PEERS - 1)), dma((2, PEERS - 1)), dma((2, PEERS - 1)), dma((2, PEERS - 1)),
            dma((PEERS - 1,)), dma((PEERS - 1,)), dma((PAIRS,)), dma((2,)),
        ],
        compiler_params=pltpu.CompilerParams(
            collective_id=0, has_side_effects=True, vmem_limit_bytes=60 << 20),
        name="marchenko",
    )(reflection, dw, fa, jnp.asarray(inv), jnp.asarray(fwd))
    out = out.reshape(2, 2, PEERS, PAIRS, 2, 2, C4, BLOCK).transpose(0, 7, 3, 4, 5, 1, 2, 6)
    out = out.reshape(2, BLOCK, FDEV, 2 * 2 * PEERS * C4)
    return (out[0], out[1])


def solution(mesh):
    in_specs = (P(None, "freq", None, "src"), P("src", "freq", None), P(("src", "freq"), None))
    out_specs = (P("src", "freq", None), P("src", "freq", None))
    return jax.shard_map(local, mesh=mesh, in_specs=in_specs, out_specs=out_specs, check_vma=False)
```

time: 550 us -> 342 us (0.62)
  Pallas kernels: 0 us -> 332 us
  waiting for transfers between devices: 309 us -> 0 us
  blocking collectives: 88.1 us -> 0 us
  local copies, waits for them, and re-layouts: 70.4 us -> 8.88 us
  matrix products: 51.2 us -> 0 us
  between operations: 14.2 us -> 0.7 us
  starting transfers between devices: 10.3 us -> 0 us
    pallas_call x0 -> x1, Pallas kernels: none -> 332 us  [local(): pl.pallas_call(kernel, out_shape=jax.ShapeDtypeStruct((2, 2, PEERS, PAIRS...]
    unnamed x8 -> x0, waiting for transfers between devices: 292 us -> none
    all_to_all x6 -> x0, blocking collectives: 88.1 us -> none  [the longest x3 49.6 us: to_owners(): lax.all_to_all(summed, 'freq', split_axis=0, concat_axis=1, tiled=True)]
    unnamed x19 -> x4, local copies, waits for them, and re-layouts: 57.8 us -> 5.11 us
    dot_general x8 -> x0, matrix products: 51.2 us -> none  [the longest x4 44 us: to_owners(): jnp.einsum('pfrs,psfk->rfk', reflection, operand, preferred_element_type=...]
    all_to_all x2 -> x0, waiting for transfers between devices: 16.4 us -> none  [the longest x1 8.63 us: to_groups(): lax.all_to_all(spectrum.astype(jnp.bfloat16), 'freq', split_axis=1, conca...]
    all_to_all x2 -> x0, starting transfers between devices: 10.1 us -> none  [the longest x1 6.61 us: to_owners(): lax.all_to_all(summed, 'freq', split_axis=0, concat_axis=1, tiled=True)]
    convert_element_type x11 -> x0, local copies, waits for them, and re-layouts: 6.41 us -> none  [the longest x8 3.66 us: to_groups(): spectrum.astype(jnp.bfloat16)]
  transfers between devices with their start and end apart: 6 -> 0, of which waited for: 6 -> 0; matrix products, arithmetic and copies ran while one was open for 1% -> 0% of each run, Pallas kernels for 0% -> 0%
where the time goes in v1:
time: 342 us
  Pallas kernels  332 us (97%)
  local copies, waits for them, and re-layouts  8.88 us (3%)
    pallas_call x1, Pallas kernels, local(): pl.pallas_call(kernel, out_shape=jax.ShapeDtypeStruct((2, 2, PEERS, PAIRS...  332 us

profile of v1, /device:TPU:0, one launch (start us, length us, event | category | flops | bytes accessed | tf_op | source)
XLA Modules:
  0.0 342.0 jit_solution(9209173576623468991)
XLA Ops:
  0.6 0.8 copy.12
  1.5 0.1 tile.12
  1.6 0.6 broadcast_select_fusion.fa
  2.2 1.6 copy.10
  3.8 1.2 copy.11
  5.1 331.8 %marchenko.1 = f32[2,2,8,8,16,128]{5,4,3,2,1,0:T(8,128)} custom-call(bf16[2,16,2048,128]{3,2,1,0:T(8,128)(2,1)} %r_hbm.1, f32[2,8,8,16,128]{4,3,2,1,0:T(8,128)} %bitcast.18, f32[8,8,128]{2,1,0:T(8,128)} %broadcast_select_fusion.fa, bf16[1536,1024]{1,0:T(8,128)(2,1)} %constant.30.clone.inv_hbm, bf16[1024,1536]{1,0:T(8,128)(2,1)} %constant.31.clone.fwd_hbm), custom_call_target="tpu_custom_call" | custom-call | tf_op jit(solution)/shard_map/marchenko/pallas_call | solution.py:282
  336.9 2.2 copy.19
  339.1 0.2 fusion.1
  339.3 1.4 copy.17
  340.7 1.4 copy.16
  (5 shorter events, 0.0 us)

commit v2 on v1

v2 whole, which is shorter than its diff:
```python
import functools
import math

import jax
import jax.numpy as jnp
import ml_dtypes
import numpy as np
from jax import lax
from jax.experimental import pallas as pl
from jax.experimental.pallas import tpu as pltpu
from jax.sharding import PartitionSpec as P

NT = 512
ITERS = 2
APPS = 2 * ITERS
NFREQ = 128
PEERS = 8
FDEV = 16
PAIRS = FDEV // 2
BLOCK = 128
C4 = 4
ROWS = 64
CUT = 192
TS = 2 * CUT
SLOTS = 16
CSLOTS = 8
D2, D3, D4, D5 = 2, 6, 10, 14
HALF_TICKS = 19
APP_TICKS = 38
WINDOW_AT = 32
UPDATE_AT = 37
MINUS_AT = (APPS - 2) * APP_TICKS + HALF_TICKS + UPDATE_AT + 1
BATCHES = ((0, 6), (6, 2))
MESH = pl.DeviceIdType.MESH
BF = jnp.bfloat16
F32 = jnp.float32


def tables():
    freqs = np.arange(1, NFREQ + 1, dtype=np.int32)
    times = np.concatenate([np.arange(CUT), np.arange(NT - CUT, NT)]).astype(np.int32)
    phase = ((freqs[:, None] * times[None, :]) % NT).astype(np.float32) * np.float32(2.0 * math.pi / NT)
    cosine, sine = np.cos(phase), np.sin(phase)
    inverse = np.stack([cosine * np.float32(2.0 / NT), -sine * np.float32(2.0 / NT)]).astype(ml_dtypes.bfloat16)
    forward = np.stack([cosine, -sine]).astype(ml_dtypes.bfloat16)
    inv = np.zeros((TS, NFREQ, 2, C4), ml_dtypes.bfloat16)
    fwd = np.zeros((NFREQ, 2, C4, TS), ml_dtypes.bfloat16)
    inv[:, :, :, 0] = inverse.transpose(2, 1, 0)
    fwd[:, :, 0, :] = forward.transpose(1, 0, 2)
    return inv.reshape(TS, NFREQ * 2 * C4), fwd.reshape(NFREQ * 2 * C4, TS)


def kernel(r_hbm, wave, fa, inv_hbm, fwd_hbm, minus, plus,
           r, inv, fwd, w, p, c_in, t, a_in, b_in, u, y_in, f, g_in, h, v_in, fa_in, wn, held, dw, out,
           ss, rs, gss, grs, hss, hrs, fss, frs, lsem, tsem):
    me = lax.axis_index("freq")
    src = lax.axis_index("src")
    core = lax.rem(src, 2)
    x = lax.rem(src // 2, 4)
    y = src // 8

    def at_src(yy, xx, cc):
        return (me, (yy * 4 + xx) * 2 + cc)

    right = lax.rem(x + 1, 4)
    left = lax.rem(x + 3, 4)
    to_core = at_src(y, x, 1 - core)
    to_right = at_src(y, right, core)
    to_left = at_src(y, left, core)
    to_y = at_src(1 - y, x, core)
    peers = [lax.rem(me + i, PEERS) for i in range(1, PEERS)]

    def load_r(k):
        part = pl.ds(2 * k, 2)
        return pltpu.make_async_copy(r_hbm.at[:, part], r.at[:, part], lsem.at[k])

    def load_tables():
        return (pltpu.make_async_copy(inv_hbm, inv.at[pl.ds(0, TS)], tsem.at[0]),
                pltpu.make_async_copy(fwd_hbm, fwd.at[:, pl.ds(0, TS)], tsem.at[1]))

    for k in range(PAIRS):
        load_r(k).start()
    for copy in load_tables():
        copy.start()

    barrier = pltpu.get_barrier_semaphore()
    for d in [to_core, to_right, to_left, to_y] + [(q, src) for q in peers]:
        pl.semaphore_signal(barrier, inc=1, device_id=d, device_id_type=MESH)
    pl.semaphore_wait(barrier, 4 + PEERS - 1)

    def remote(source, target, send, recv, device):
        return pltpu.make_async_remote_copy(
            src_ref=source, dst_ref=target, send_sem=send, recv_sem=recv, device_id=device, device_id_type=MESH)

    def core_copy(k):
        s = lax.rem(k, CSLOTS)
        return remote(p.at[s, 1 - core], c_in.at[s], ss.at[0, s], rs.at[0, s], to_core)

    def a_copies(k):
        s = lax.rem(k, SLOTS)
        return (remote(t.at[s, 2, 0], a_in.at[s, 0], ss.at[1, s], rs.at[1, s], to_right),
                remote(t.at[s, 2, 1], a_in.at[s, 1], ss.at[2, s], rs.at[2, s], to_left))

    def b_copies(k):
        s = lax.rem(k, SLOTS)
        return (remote(t.at[s, 1], b_in.at[s, 0], ss.at[3, s], rs.at[3, s], to_right),
                remote(t.at[s, 3], b_in.at[s, 1], ss.at[4, s], rs.at[4, s], to_left))

    def y_copy(k):
        s = lax.rem(k, SLOTS)
        return remote(u.at[s, 1], y_in.at[s], ss.at[5, s], rs.at[5, s], to_y)

    def fa_copy(i):
        return remote(fa.at[peers[i]], fa_in.at[me], fss.at[i], frs.at[i], (peers[i], src))

    def g_copy(half, i, b):
        part = pl.ds(*BATCHES[b])
        return remote(f.at[half, peers[i], part], g_in.at[half, me, part],
                      gss.at[half, b, i], grs.at[half, b, i], (peers[i], src))

    def h_copy(half, i):
        return remote(h.at[half, peers[i]], v_in.at[half, me], hss.at[half, i], hrs.at[half, i], (peers[i], src))

    for i in range(PEERS - 1):
        fa_copy(i).start()
    fa_in[me] = fa[me]

    low = lax.broadcasted_iota(jnp.int32, (PEERS, 2 * C4, BLOCK), 1) < C4

    def expand(c):
        for i in range(NFREQ * 2 * C4 // BLOCK):
            lanes = slice(i * BLOCK, (i + 1) * BLOCK)
            inv[c * TS:(c + 1) * TS, lanes] = pltpu.roll(inv[0:TS, lanes].astype(F32), c, 1).astype(BF)
        for i in range(TS // BLOCK):
            first = fwd[:, i * BLOCK:(i + 1) * BLOCK].astype(F32).reshape(NFREQ, 2 * C4, BLOCK)
            fwd[:, c * TS + i * BLOCK:c * TS + (i + 1) * BLOCK] = pltpu.roll(first, c, 1).reshape(-1, BLOCK).astype(BF)

    def stack_rows(half, part, freq, sign):
        turned = pltpu.roll(part, C4, 1)
        turned = jnp.where(low, -sign * turned, sign * turned)
        w[half, freq, :, 0:BLOCK] = part.reshape(ROWS, BLOCK).astype(BF)
        w[half, freq, :, BLOCK:2 * BLOCK] = turned.reshape(ROWS, BLOCK).astype(BF)

    def first_rows(freq):
        both = jnp.transpose(wave[pl.ds(freq, BLOCK, stride=FDEV), :])
        re = both[0:ROWS].reshape(PEERS, 2 * C4, BLOCK)
        im = both[ROWS:2 * ROWS].reshape(PEERS, 2 * C4, BLOCK)
        for half, part in ((0, jnp.where(low, re, pltpu.roll(im, C4, 1))), (1, jnp.where(low, pltpu.roll(re, C4, 1), im))):
            dw[half, freq] = part
            stack_rows(half, part, freq, 1.0)

    def emit(odd, target, freq):
        first, second = out[odd, 0, freq], out[odd, 1, freq]
        re = jnp.where(low, first, pltpu.roll(second, C4, 1)).reshape(ROWS, BLOCK)
        im = jnp.where(low, pltpu.roll(first, C4, 1), second).reshape(ROWS, BLOCK)
        target[pl.ds(freq, BLOCK, stride=FDEV), :] = jnp.transpose(jnp.concatenate([re, im], axis=0))

    def matmul(k):
        s = lax.rem(k, CSLOTS)
        freq = lax.rem(k, FDEV)
        lhs = w[lax.rem(k // FDEV, 2), freq]
        for xr in range(4):
            for yr in range(2):
                yy = y if yr == 0 else 1 - y
                start = pl.multiple_of((yy * 4 + lax.rem(x + xr, 4)) * 2 * BLOCK, 2 * BLOCK)
                rows = pl.ds(start, 2 * BLOCK)
                rhs = jnp.concatenate([r[0, freq, rows, :], r[1, freq, rows, :]], axis=1)
                term = lax.dot_general(lhs, rhs, (((1,), (1,)), ((), ())), preferred_element_type=F32).astype(BF)
                p[s, 0, xr, yr] = term[:, 0:BLOCK]
                p[s, 1, xr, yr] = term[:, BLOCK:2 * BLOCK]

    def window(n):
        half = lax.rem(n, 2)
        for b in range(len(BATCHES)):
            for i in range(PEERS - 1):
                g_copy(half, i, b).wait()
        spectrum = g_in[half].reshape(NFREQ * 2 * C4, BLOCK)
        time = lax.broadcasted_iota(jnp.int32, (TS, BLOCK), 0)
        time = jnp.where(time < CUT, time, time + (NT - TS)).astype(F32)
        for c in range(C4):
            signal = jnp.dot(inv[c * TS:(c + 1) * TS, :], spectrum, preferred_element_type=F32)
            limit = fa_in[0, pl.ds(half * C4 + c, 1), :]
            for q in range(1, PEERS):
                limit = limit + fa_in[q, pl.ds(half * C4 + c, 1), :]
            keep = (time < limit) | (time > NT - limit)
            wn[c * TS:(c + 1) * TS, :] = jnp.where(keep, signal, 0.0).astype(BF)
        for i, q in enumerate(peers + [me]):
            rows = pl.ds(pl.multiple_of(q * BLOCK, BLOCK), BLOCK)
            back = jnp.dot(fwd[rows, :], wn[...], preferred_element_type=F32)
            back = back.astype(BF).reshape(PAIRS, 16, BLOCK)
            if i < PEERS - 1:
                h[half, q] = back
                h_copy(half, i).start()
            else:
                v_in[half, me] = back

    def update(n):
        half = lax.rem(n, 2)
        app = n // 2
        odd = lax.rem(app, 2)
        flag = odd.astype(F32)
        sign = 2.0 * flag - 1.0
        for i in range(PEERS - 1):
            h_copy(half, i).wait()

        def one(pair, carry):
            both = v_in[half, :, pair].astype(F32)
            for q in range(2):
                freq = 2 * pair + q
                value = both[:, 2 * C4 * q:2 * C4 * (q + 1), :] + flag * dw[half, freq]
                out[odd, half, freq] = value
                stack_rows(half, value, freq, sign)
            return carry

        lax.fori_loop(0, PAIRS, one, 0)

    def chunk(k, delay):
        k = k + APP_TICKS - delay
        app = k // APP_TICKS - 1
        at = lax.rem(k, APP_TICKS)
        half = jnp.where(at >= HALF_TICKS, 1, 0)
        at = at - half * HALF_TICKS
        return (app >= 0) & (app < APPS) & (at < FDEV), (app * 2 + half) * FDEV + at

    def trace(k, delay):
        some, j = chunk(k, delay)
        return some & (lax.rem(j, FDEV) == 0), j // FDEV

    def tick(k, carry):
        some5, j5 = chunk(k, D5)
        some4, j4 = chunk(k, D4)
        some3, j3 = chunk(k, D3)
        some2, j2 = chunk(k, D2)
        some1, j1 = chunk(k, 0)
        some_w, nw = trace(k, WINDOW_AT)
        some_u, nu = trace(k, UPDATE_AT)

        @pl.when(some5)
        def _():
            s = lax.rem(j5, SLOTS)
            freq = lax.rem(j5, FDEV)
            odd, pair = lax.rem(freq, 2), freq // 2
            half = lax.rem(j5 // FDEV, 2)
            y_copy(j5).wait()
            held[odd] = u[s, 0].astype(F32) + y_in[s].astype(F32)

            @pl.when(odd == 1)
            def _():
                total = held[...].reshape(2, PEERS, 2 * C4, BLOCK)
                f[half, :, pair] = jnp.concatenate([total[0], total[1]], axis=1).astype(BF)

            for b, (first, length) in enumerate(BATCHES):
                @pl.when((odd == 1) & (pair == first + length - 1))
                def _():
                    for i in range(PEERS - 1):
                        g_copy(half, i, b).start()
                    part = pl.ds(first, length)
                    g_in[half, me, part] = f[half, me, part]

        @pl.when(some4)
        def _():
            s = lax.rem(j4, SLOTS)
            for copy in b_copies(j4):
                copy.wait()
            u[s, 1] = (t[s, 0, 1].astype(F32) + b_in[s, 0, 1].astype(F32) + b_in[s, 1, 1].astype(F32)).astype(BF)
            y_copy(j4).start()
            u[s, 0] = (t[s, 0, 0].astype(F32) + b_in[s, 0, 0].astype(F32) + b_in[s, 1, 0].astype(F32)).astype(BF)

        @pl.when(some3)
        def _():
            s = lax.rem(j3, SLOTS)
            for copy in a_copies(j3):
                copy.wait()
            t[s, 1, 0] = (t[s, 1, 0].astype(F32) + a_in[s, 0].astype(F32)).astype(BF)
            t[s, 3, 1] = (t[s, 3, 1].astype(F32) + a_in[s, 1].astype(F32)).astype(BF)
            for copy in b_copies(j3):
                copy.start()

        @pl.when(some2)
        def _():
            s = lax.rem(j2, SLOTS)
            cs = lax.rem(j2, CSLOTS)
            core_copy(j2).wait()
            for xr in (2, 1, 3, 0):
                t[s, xr] = (p[cs, core, xr].astype(F32) + c_in[cs, xr].astype(F32)).astype(BF)
                if xr == 2:
                    for copy in a_copies(j2):
                        copy.start()

        @pl.when((k < FDEV) & (lax.rem(k, 2) == 0))
        def _():
            load_r(k // 2).wait()

        @pl.when(k < FDEV)
        def _():
            first_rows(k)

        @pl.when(some1)
        def _():
            matmul(j1)
            core_copy(j1).start()

        @pl.when(k == FDEV)
        def _():
            for copy in load_tables():
                copy.wait()
            for i in range(PEERS - 1):
                fa_copy(i).wait()

        for c in range(1, C4):
            @pl.when(k == FDEV + 2 * c)
            def _():
                expand(c)

        @pl.when(some_w)
        def _():
            window(nw)

        @pl.when(some_u)
        def _():
            update(nu)

        @pl.when((k >= MINUS_AT) & (k < MINUS_AT + FDEV))
        def _():
            emit(0, minus, k - MINUS_AT)

        return carry

    lax.fori_loop(0, (APPS - 1) * APP_TICKS + HALF_TICKS + UPDATE_AT + 1, tick, 0)

    def last(freq, carry):
        emit(1, plus, freq)
        return carry

    lax.fori_loop(0, FDEV, last, 0)


def local(reflection, direct_wave, first_arrival):
    me = lax.axis_index("freq")
    inv, fwd = tables()
    wave = direct_wave.reshape(BLOCK * FDEV, BLOCK)
    fa = first_arrival.astype(F32).reshape(16, PEERS, 2 * C4).transpose(1, 2, 0)
    fa = jnp.where(jnp.arange(BLOCK) // 16 == me, jnp.tile(fa, (1, 1, PEERS)), 0.0)
    vmem = pl.BlockSpec(memory_space=pltpu.VMEM)
    hbm = pl.BlockSpec(memory_space=pl.ANY)
    dma = pltpu.SemaphoreType.DMA
    unit = (ROWS, BLOCK)
    outs = pl.pallas_call(
        kernel,
        out_shape=[jax.ShapeDtypeStruct(wave.shape, F32)] * 2,
        in_specs=[hbm, vmem, vmem, hbm, hbm],
        out_specs=[vmem, vmem],
        scratch_shapes=[
            pltpu.VMEM(reflection.shape, BF),
            pltpu.VMEM((C4 * TS, inv.shape[1]), BF),
            pltpu.VMEM((fwd.shape[0], C4 * TS), BF),
            pltpu.VMEM((2, FDEV, ROWS, 2 * BLOCK), BF),
            pltpu.VMEM((CSLOTS, 2, 4, 2) + unit, BF),
            pltpu.VMEM((CSLOTS, 4, 2) + unit, BF),
            pltpu.VMEM((SLOTS, 4, 2) + unit, BF),
            pltpu.VMEM((SLOTS, 2) + unit, BF),
            pltpu.VMEM((SLOTS, 2, 2) + unit, BF),
            pltpu.VMEM((SLOTS, 2) + unit, BF),
            pltpu.VMEM((SLOTS,) + unit, BF),
            pltpu.VMEM((2, PEERS, PAIRS, 16, BLOCK), BF),
            pltpu.VMEM((2, PEERS, PAIRS, 16, BLOCK), BF),
            pltpu.VMEM((2, PEERS, PAIRS, 16, BLOCK), BF),
            pltpu.VMEM((2, PEERS, PAIRS, 16, BLOCK), BF),
            pltpu.VMEM((PEERS, 2 * C4, BLOCK), F32),
            pltpu.VMEM((C4 * TS, BLOCK), BF),
            pltpu.VMEM((2, ROWS, BLOCK), F32),
            pltpu.VMEM((2, FDEV, PEERS, 2 * C4, BLOCK), F32),
            pltpu.VMEM((2, 2, FDEV, PEERS, 2 * C4, BLOCK), F32),
            dma((6, SLOTS)), dma((6, SLOTS)),
            dma((2, len(BATCHES), PEERS - 1)), dma((2, len(BATCHES), PEERS - 1)),
            dma((2, PEERS - 1)), dma((2, PEERS - 1)),
            dma((PEERS - 1,)), dma((PEERS - 1,)), dma((PAIRS,)), dma((2,)),
        ],
        compiler_params=pltpu.CompilerParams(
            collective_id=0, has_side_effects=True, vmem_limit_bytes=60 << 20),
        name="marchenko",
    )(reflection, wave, fa, jnp.asarray(inv), jnp.asarray(fwd))
    return tuple(o.reshape(direct_wave.shape) for o in outs)


def solution(mesh):
    in_specs = (P(None, "freq", None, "src"), P("src", "freq", None), P(("src", "freq"), None))
    out_specs = (P("src", "freq", None), P("src", "freq", None))
    return jax.shard_map(local, mesh=mesh, in_specs=in_specs, out_specs=out_specs, check_vma=False)
```

time: 342 us -> 222 us (0.65)
  Pallas kernels: 332 us -> 215 us
  local copies, waits for them, and re-layouts: 8.88 us -> 5.45 us
    pallas_call x1, Pallas kernels: 332 us -> 215 us  [local(): pl.pallas_call(kernel, out_shape=[jax.ShapeDtypeStruct(wave.shape, F32)]...]
where the time goes in v2:
time: 222 us; the launch traced here: 221 us
  Pallas kernels  215 us (97%)
  local copies, waits for them, and re-layouts  5.45 us (2%)
    pallas_call x1, Pallas kernels, local(): pl.pallas_call(kernel, out_shape=[jax.ShapeDtypeStruct(wave.shape, F32)]...  215 us
    unnamed x3, local copies, waits for them, and re-layouts  5.3 us

profile of v2, /device:TPU:0, one launch (start us, length us, event | category | flops | bytes accessed | tf_op | source)
XLA Modules:
  0.0 221.3 jit_solution(4934589871153274692)
XLA Ops:
  0.6 0.8 copy.8
  1.5 0.1 tile.10
  1.6 0.6 broadcast_select_fusion.fa
  2.2 214.5 %marchenko.1 = (f32[2048,128]{1,0:T(8,128)}, f32[2048,128]{1,0:T(8,128)}) custom-call(bf16[2,16,2048,128]{3,2,1,0:T(8,128)(2,1)} %r_hbm.1, f32[2048,128]{1,0:T(8,128)} %bitcast.9, f32[8,8,128]{2,1,0:T(8,128)} %broadcast_select_fusion.fa, bf16[384,1024]{1,0:T(8,128)(2,1)} %constant.30.clone.inv_hbm, bf16[1024,384]{1,0:T(8,128)(2,1)} %constant.31.clone.fwd_hbm), custom_call_target="tpu_custom_call" | custom-call | tf_op jit(solution)/shard_map/marchenko/pallas_call | solution.py:348
  216.8 2.3 %copy.11 = f32[128,16,128]{2,1,0:T(8,128)} copy(f32[128,16,128]{2,1,0:T(8,128)} %bitcast.11) | data formatting | bytes 2097152
  219.0 2.3 %copy.12 = f32[128,16,128]{2,1,0:T(8,128)} copy(f32[128,16,128]{2,1,0:T(8,128)} %bitcast.10) | data formatting | bytes 2097152
  (3 shorter events, 0.0 us)

commit v3 on v2

--- a/solution.py
+++ b/solution.py
@@ -22,14 +22,18 @@
 ROWS = 64
 CUT = 192
 TS = 2 * CUT
-SLOTS = 16
-CSLOTS = 8
-D2, D3, D4, D5 = 2, 6, 10, 14
-HALF_TICKS = 19
-APP_TICKS = 38
-WINDOW_AT = 32
-UPDATE_AT = 37
-MINUS_AT = (APPS - 2) * APP_TICKS + HALF_TICKS + UPDATE_AT + 1
+SLOTS = PAIRS
+PERIOD = 19
+AT_MATMUL = (0, 2, 3, 4, 6, 9, 11, 13)
+AT_CORE = (3, 4, 6, 7, 9, 12, 14, 15)
+AT_NEAR = (5, 8, 10, 12, 13, 16, 17, 20)
+AT_RING = (11, 13, 15, 16, 17, 21, 23, 24)
+AT_LAST = (16, 18, 19, 21, 24, 25, 26, 27)
+AT_WINDOW = 31
+AT_UPDATE = 37
+HALVES = 2 * APPS
+TICKS = (HALVES - 1) * PERIOD + AT_UPDATE + 1
+MINUS_AT = (HALVES - 3) * PERIOD + AT_UPDATE + 1
 BATCHES = ((0, 6), (6, 2))
 MESH = pl.DeviceIdType.MESH
 BF = jnp.bfloat16
@@ -51,7 +55,7 @@
 
 
 def kernel(r_hbm, wave, fa, inv_hbm, fwd_hbm, minus, plus,
-           r, inv, fwd, w, p, c_in, t, a_in, b_in, u, y_in, f, g_in, h, v_in, fa_in, wn, held, dw, out,
+           r, inv, fwd, w, p, c_in, t, a_in, b_in, u, y_in, f, g_in, h, v_in, fa_in, wn, dw, out,
            ss, rs, gss, grs, hss, hrs, fss, frs, lsem, tsem):
     me = lax.axis_index("freq")
     src = lax.axis_index("src")
@@ -93,7 +97,7 @@
             src_ref=source, dst_ref=target, send_sem=send, recv_sem=recv, device_id=device, device_id_type=MESH)
 
     def core_copy(k):
-        s = lax.rem(k, CSLOTS)
+        s = lax.rem(k, SLOTS)
         return remote(p.at[s, 1 - core], c_in.at[s], ss.at[0, s], rs.at[0, s], to_core)
 
     def a_copies(k):
@@ -156,18 +160,20 @@
         target[pl.ds(freq, BLOCK, stride=FDEV), :] = jnp.transpose(jnp.concatenate([re, im], axis=0))
 
     def matmul(k):
-        s = lax.rem(k, CSLOTS)
-        freq = lax.rem(k, FDEV)
-        lhs = w[lax.rem(k // FDEV, 2), freq]
-        for xr in range(4):
-            for yr in range(2):
-                yy = y if yr == 0 else 1 - y
-                start = pl.multiple_of((yy * 4 + lax.rem(x + xr, 4)) * 2 * BLOCK, 2 * BLOCK)
-                rows = pl.ds(start, 2 * BLOCK)
-                rhs = jnp.concatenate([r[0, freq, rows, :], r[1, freq, rows, :]], axis=1)
-                term = lax.dot_general(lhs, rhs, (((1,), (1,)), ((), ())), preferred_element_type=F32).astype(BF)
-                p[s, 0, xr, yr] = term[:, 0:BLOCK]
-                p[s, 1, xr, yr] = term[:, BLOCK:2 * BLOCK]
+        s = lax.rem(k, SLOTS)
+        half = lax.rem(k // PAIRS, 2)
+        for q in range(2):
+            freq = 2 * s + q
+            lhs = w[half, freq]
+            for xr in range(4):
+                for yr in range(2):
+                    yy = y if yr == 0 else 1 - y
+                    start = pl.multiple_of((yy * 4 + lax.rem(x + xr, 4)) * 2 * BLOCK, 2 * BLOCK)
+                    rows = pl.ds(start, 2 * BLOCK)
+                    rhs = jnp.concatenate([r[0, freq, rows, :], r[1, freq, rows, :]], axis=1)
+                    term = lax.dot_general(lhs, rhs, (((1,), (1,)), ((), ())), preferred_element_type=F32).astype(BF)
+                    p[s, 0, xr, yr, q] = term[:, 0:BLOCK]
+                    p[s, 1, xr, yr, q] = term[:, BLOCK:2 * BLOCK]
 
     def window(n):
         half = lax.rem(n, 2)
@@ -214,43 +220,38 @@
 
         lax.fori_loop(0, PAIRS, one, 0)
 
-    def chunk(k, delay):
-        k = k + APP_TICKS - delay
-        app = k // APP_TICKS - 1
-        at = lax.rem(k, APP_TICKS)
-        half = jnp.where(at >= HALF_TICKS, 1, 0)
-        at = at - half * HALF_TICKS
-        return (app >= 0) & (app < APPS) & (at < FDEV), (app * 2 + half) * FDEV + at
-
-    def trace(k, delay):
-        some, j = chunk(k, delay)
-        return some & (lax.rem(j, FDEV) == 0), j // FDEV
+    def chunk(k, at):
+        since = k - at[0]
+        n = jnp.maximum(since, 0) // PERIOD
+        since = since - n * PERIOD
+        some, j = since == 0, jnp.int32(0)
+        for other in at[1:]:
+            some = some | (since == other - at[0])
+            j = j + jnp.where(since >= other - at[0], 1, 0)
+        return some & (n < HALVES), n * PAIRS + j
+
+    def trace(k, at):
+        n = jnp.maximum(k - at, 0) // PERIOD
+        return (k - at == n * PERIOD) & (n < HALVES), n
 
     def tick(k, carry):
-        some5, j5 = chunk(k, D5)
-        some4, j4 = chunk(k, D4)
-        some3, j3 = chunk(k, D3)
-        some2, j2 = chunk(k, D2)
-        some1, j1 = chunk(k, 0)
-        some_w, nw = trace(k, WINDOW_AT)
-        some_u, nu = trace(k, UPDATE_AT)
+        some5, j5 = chunk(k, AT_LAST)
+        some4, j4 = chunk(k, AT_RING)
+        some3, j3 = chunk(k, AT_NEAR)
+        some2, j2 = chunk(k, AT_CORE)
+        some1, j1 = chunk(k, AT_MATMUL)
+        some_w, nw = trace(k, AT_WINDOW)
+        some_u, nu = trace(k, AT_UPDATE)
 
         @pl.when(some5)
         def _():
             s = lax.rem(j5, SLOTS)
-            freq = lax.rem(j5, FDEV)
-            odd, pair = lax.rem(freq, 2), freq // 2
-            half = lax.rem(j5 // FDEV, 2)
+            half = lax.rem(j5 // PAIRS, 2)
             y_copy(j5).wait()
-            held[odd] = u[s, 0].astype(F32) + y_in[s].astype(F32)
-
-            @pl.when(odd == 1)
-            def _():
-                total = held[...].reshape(2, PEERS, 2 * C4, BLOCK)
-                f[half, :, pair] = jnp.concatenate([total[0], total[1]], axis=1).astype(BF)
-
+            total = (u[s, 0].astype(F32) + y_in[s].astype(F32)).reshape(2, PEERS, 2 * C4, BLOCK)
+            f[half, :, s] = jnp.concatenate([total[0], total[1]], axis=1).astype(BF)
             for b, (first, length) in enumerate(BATCHES):
-                @pl.when((odd == 1) & (pair == first + length - 1))
+                @pl.when(s == first + length - 1)
                 def _():
                     for i in range(PEERS - 1):
                         g_copy(half, i, b).start()
@@ -279,21 +280,18 @@
         @pl.when(some2)
         def _():
             s = lax.rem(j2, SLOTS)
-            cs = lax.rem(j2, CSLOTS)
             core_copy(j2).wait()
             for xr in (2, 1, 3, 0):
-                t[s, xr] = (p[cs, core, xr].astype(F32) + c_in[cs, xr].astype(F32)).astype(BF)
+                t[s, xr] = (p[s, core, xr].astype(F32) + c_in[s, xr].astype(F32)).astype(BF)
                 if xr == 2:
                     for copy in a_copies(j2):
                         copy.start()
 
-        @pl.when((k < FDEV) & (lax.rem(k, 2) == 0))
-        def _():
-            load_r(k // 2).wait()
-
-        @pl.when(k < FDEV)
-        def _():
-            first_rows(k)
+        @pl.when(some1 & (j1 < PAIRS))
+        def _():
+            load_r(j1).wait()
+            for q in range(2):
+                first_rows(2 * j1 + q)
 
         @pl.when(some1)
         def _():
@@ -326,7 +324,7 @@
 
         return carry
 
-    lax.fori_loop(0, (APPS - 1) * APP_TICKS + HALF_TICKS + UPDATE_AT + 1, tick, 0)
+    lax.fori_loop(0, TICKS, tick, 0)
 
     def last(freq, carry):
         emit(1, plus, freq)
@@ -344,7 +342,7 @@
     vmem = pl.BlockSpec(memory_space=pltpu.VMEM)
     hbm = pl.BlockSpec(memory_space=pl.ANY)
     dma = pltpu.SemaphoreType.DMA
-    unit = (ROWS, BLOCK)
+    unit = (2, ROWS, BLOCK)
     outs = pl.pallas_call(
         kernel,
         out_shape=[jax.ShapeDtypeStruct(wave.shape, F32)] * 2,
@@ -355,8 +353,8 @@
             pltpu.VMEM((C4 * TS, inv.shape[1]), BF),
             pltpu.VMEM((fwd.shape[0], C4 * TS), BF),
             pltpu.VMEM((2, FDEV, ROWS, 2 * BLOCK), BF),
-            pltpu.VMEM((CSLOTS, 2, 4, 2) + unit, BF),
-            pltpu.VMEM((CSLOTS, 4, 2) + unit, BF),
+            pltpu.VMEM((SLOTS, 2, 4, 2) + unit, BF),
+            pltpu.VMEM((SLOTS, 4, 2) + unit, BF),
             pltpu.VMEM((SLOTS, 4, 2) + unit, BF),
             pltpu.VMEM((SLOTS, 2) + unit, BF),
             pltpu.VMEM((SLOTS, 2, 2) + unit, BF),
@@ -368,7 +366,6 @@
             pltpu.VMEM((2, PEERS, PAIRS, 16, BLOCK), BF),
             pltpu.VMEM((PEERS, 2 * C4, BLOCK), F32),
             pltpu.VMEM((C4 * TS, BLOCK), BF),
-            pltpu.VMEM((2, ROWS, BLOCK), F32),
             pltpu.VMEM((2, FDEV, PEERS, 2 * C4, BLOCK), F32),
             pltpu.VMEM((2, 2, FDEV, PEERS, 2 * C4, BLOCK), F32),
             dma((6, SLOTS)), dma((6, SLOTS)),

time: 222 us -> 214 us (0.964)
  Pallas kernels: 215 us -> 207 us
    pallas_call x1, Pallas kernels: 215 us -> 207 us  [local(): pl.pallas_call(kernel, out_shape=[jax.ShapeDtypeStruct(wave.shape, F32)]...]
where the time goes in v3:
time: 214 us; the launch traced here: 213 us
  Pallas kernels  207 us (97%)
  local copies, waits for them, and re-layouts  5.45 us (3%)
    pallas_call x1, Pallas kernels, local(): pl.pallas_call(kernel, out_shape=[jax.ShapeDtypeStruct(wave.shape, F32)]...  207 us
    unnamed x3, local copies, waits for them, and re-layouts  5.3 us

profile of v3, /device:TPU:0, one launch (start us, length us, event | category | flops | bytes accessed | tf_op | source)
XLA Modules:
  0.0 213.4 jit_solution(14221207840119894403)
XLA Ops:
  0.6 0.8 copy.8
  1.5 0.1 tile.10
  1.6 0.6 broadcast_select_fusion.fa
  2.2 206.7 %marchenko.1 = (f32[2048,128]{1,0:T(8,128)}, f32[2048,128]{1,0:T(8,128)}) custom-call(bf16[2,16,2048,128]{3,2,1,0:T(8,128)(2,1)} %r_hbm.1, f32[2048,128]{1,0:T(8,128)} %bitcast.9, f32[8,8,128]{2,1,0:T(8,128)} %broadcast_select_fusion.fa, bf16[384,1024]{1,0:T(8,128)(2,1)} %constant.30.clone.inv_hbm, bf16[1024,384]{1,0:T(8,128)(2,1)} %constant.31.clone.fwd_hbm), custom_call_target="tpu_custom_call" | custom-call | tf_op jit(solution)/shard_map/marchenko/pallas_call | solution.py:346
  208.9 2.3 %copy.11 = f32[128,16,128]{2,1,0:T(8,128)} copy(f32[128,16,128]{2,1,0:T(8,128)} %bitcast.11) | data formatting | bytes 2097152
  211.1 2.3 %copy.12 = f32[128,16,128]{2,1,0:T(8,128)} copy(f32[128,16,128]{2,1,0:T(8,128)} %bitcast.10) | data formatting | bytes 2097152
  (3 shorter events, 0.0 us)
